TPU v7x, 32 devices: a whole 2x2x4 slice. The times are simulated.
32 devices in a mesh: grp: 2 (over x), head: 16 (over z, y, core).
Axes of the slice: x: 2, y: 2, z: 4, core: 2. Of those that a mesh axis runs over, the one named last changes fastest.
Arguments:
- queries: bfloat16 [2048, 2, 16, 256], P('head', 'grp'), parts along dimension 1, may hold values from -12 to 12
- new_kv: bfloat16 [2048, 2, 2, 512], P('head', 'grp'), parts along dimension 1, may hold values from -4 to 4
- cache: bfloat16 [32, 256, 512], P(('grp', 'head')), parts along dimension 0, may hold values from -12 to 12
- resid: bfloat16 [2048, 2, 2048], P('head', 'grp'), parts along dimension 1, may hold values from -6 to 6
- w_out: bfloat16 [16, 256, 2048], P(None, 'head'), may hold values from -0.375 to 0.375
- norm_gain: float32 [2048], replicated, may hold values from 0.1 to 1.9
- expert_ids: int32 [2048, 2, 2], P('head', 'grp'), parts along dimension 1, may hold values from 0 to 15, all different within a row; in each aligned block of 128 rows (0 to 127, 128 to 255, ..., all dimensions but the last counted through in order) at most 32 rows name the same one
- expert_gates: float32 [2048, 2, 2], P('head', 'grp'), parts along dimension 1, may hold values from 0.2 to 1
- w_in: bfloat16 [16, 2048, 1024], P('head'), may hold values from -0.125 to 0.125
- w_down: bfloat16 [16, 512, 2048], P('head'), may hold values from -0.25 to 0.25
Outputs:
- layer_out: bfloat16 [2048, 2, 2048], P('head', 'grp'), parts along dimension 1
There are 2 independent parts, one for each index of `grp`. A program takes and returns all parts, laid end to end along the dimension named above; an argument that names none is the same for every part. Nothing has to cross between parts.
Inputs may be any that keep to these rules, and one draw needn't show every extreme that they name: `expert_ids`: rows are taken in order over positions and then sequences; in each aligned block of 128 such rows (the rows of one device) no expert is named by more than 32 rows, a bound that some block reaches. A row names 2 different experts.
All inputs are finite; a program needn't handle non-finite values.
Results may differ from a plain program's by a relative error of at most 0.009.
Values may be sent and summed in bfloat16 or wider, within the bound.
A program may use at most 128 MiB of HBM per device.

v0:
```python
import jax
import jax.numpy as jnp
from jax import lax
from jax.sharding import PartitionSpec as P

eps_norm = 1e-06


def partner_2(value, axis, stride):
    mask = 2**stride
    pairs = [(source, source ^ mask) for source in range(lax.axis_size(axis))]
    return lax.ppermute(value, axis, pairs)


def attend(query_rows_all, new_keys, new_values, cached):
    length = query_rows_all.shape[0]
    head_width = query_rows_all.shape[1]
    block_rows = min(512, length)
    score_scale = head_width ** (-0.5)
    old_keys = cached[:, :head_width]
    old_values = cached[:, head_width:]
    key_positions = jnp.arange(length, dtype=jnp.int32)

    def one_block(first_row):
        query_rows = lax.dynamic_slice_in_dim(query_rows_all, first_row, block_rows, 0)
        old_scores = (
            jnp.dot(query_rows, old_keys.T, preferred_element_type=jnp.float32) * score_scale
        )
        new_scores = (
            jnp.dot(query_rows, new_keys.T, preferred_element_type=jnp.float32) * score_scale
        )
        row_positions = first_row + jnp.arange(block_rows, dtype=jnp.int32)
        allowed = key_positions[None, :] <= row_positions[:, None]
        new_scores = jnp.where(allowed, new_scores, -jnp.inf)
        row_max = jnp.maximum(jnp.max(old_scores, 1), jnp.max(new_scores, 1))[:, None]
        old_exp = jnp.exp(old_scores - row_max)
        new_exp = jnp.exp(new_scores - row_max)
        denominator = jnp.sum(old_exp, 1) + jnp.sum(new_exp, 1)
        weighted_sum = jnp.dot(
            old_exp.astype(jnp.bfloat16), old_values, preferred_element_type=jnp.float32
        )
        weighted_sum = weighted_sum + jnp.dot(
            new_exp.astype(jnp.bfloat16), new_values, preferred_element_type=jnp.float32
        )
        return (weighted_sum / denominator[:, None]).astype(jnp.bfloat16)

    starts = jnp.arange(length // block_rows) * block_rows
    return lax.map(one_block, starts).reshape(length, head_width)


def local(queries, new_kv, cache, resid, w_out, norm_gain, expert_ids, expert_gates, w_in, w_down):
    axis_count = lax.axis_size("head")
    local_rows = queries.shape[0]
    seq_count = queries.shape[1]
    head_count = queries.shape[2]
    head_width = queries.shape[3]
    pair_heads = new_kv.shape[2]
    group_size = head_count // pair_heads
    model_width = resid.shape[2]
    row_count = local_rows * seq_count
    query_slots = queries.reshape(local_rows, axis_count, head_width)
    pair_slots = jnp.broadcast_to(
        new_kv[:, :, :, None, :], (local_rows, seq_count, pair_heads, group_size, 2 * head_width)
    )
    pair_slots = pair_slots.reshape(local_rows, axis_count, 2 * head_width)
    head_queries = lax.all_to_all(query_slots, "head", split_axis=1, concat_axis=0, tiled=True)[
        :, 0
    ]
    head_pairs = lax.all_to_all(pair_slots, "head", split_axis=1, concat_axis=0, tiled=True)[:, 0]
    cache_rows = cache[0]
    for bit_number in range(group_size.bit_length() - 1):
        partner = partner_2(cache_rows, "head", bit_number)
        cache_rows = jnp.concatenate([cache_rows, partner], 0)
    attended = attend(
        head_queries, head_pairs[:, :head_width], head_pairs[:, head_width:], cache_rows
    )
    returned = lax.all_to_all(
        attended.reshape(attended.shape[0], 1, head_width),
        "head",
        split_axis=0,
        concat_axis=1,
        tiled=True,
    )
    attn_rows = returned.reshape(row_count, head_count * head_width)
    attn_heads = attn_rows.reshape(row_count, head_count, head_width)
    projected = jnp.einsum(
        "rhi,hid->rd",
        attn_heads,
        lax.all_gather(w_out, "head", axis=1, tiled=True),
        preferred_element_type=jnp.float32,
    )
    stream = resid.reshape(row_count, model_width).astype(jnp.float32) + projected
    normed = stream * lax.rsqrt(jnp.mean(stream * stream, 1, keepdims=True) + eps_norm) * norm_gain
    normed = normed.astype(jnp.bfloat16)
    top_count = expert_ids.shape[2]
    flat_ids = expert_ids.reshape(-1)
    local_experts = w_in.shape[0]
    experts = local_experts * axis_count
    capacity = max(2, 2 * row_count * top_count // experts)
    onehot = (flat_ids[:, None] == jnp.arange(experts, dtype=jnp.int32)[None, :]).astype(jnp.int32)
    earlier = jnp.cumsum(onehot, 0) - onehot
    slot_rank = jnp.sum(earlier * onehot, 1)
    target = flat_ids * capacity + slot_rank
    repeated = jnp.repeat(normed, top_count, axis=0)
    outgoing = jnp.zeros((experts * capacity, model_width), jnp.bfloat16).at[target].set(repeated)
    outgoing = outgoing.reshape(experts, 1, capacity, model_width)
    hidden_width = w_down.shape[1]
    inner_act = jnp.einsum(
        "esmd,edf->esmf",
        lax.all_to_all(outgoing, "head", split_axis=0, concat_axis=1, tiled=True),
        w_in,
        preferred_element_type=jnp.float32,
    )
    hidden = (jax.nn.silu(inner_act[..., :hidden_width]) * inner_act[..., hidden_width:]).astype(
        jnp.bfloat16
    )
    answered = jnp.einsum(
        "esmf,efd->esmd", hidden, w_down, preferred_element_type=jnp.float32
    ).astype(jnp.bfloat16)
    returned_rows = lax.all_to_all(answered, "head", split_axis=1, concat_axis=0, tiled=True)
    picked = returned_rows.reshape(experts * capacity, model_width)[target].astype(jnp.float32)
    weighted = picked * expert_gates.reshape(-1)[:, None]
    expert_sum = weighted.reshape(row_count, top_count, model_width).sum(1)
    return (stream + expert_sum).astype(jnp.bfloat16).reshape(local_rows, seq_count, model_width)


def solution(mesh):
    return jax.shard_map(
        local,
        mesh=mesh,
        in_specs=(
            P("head", "grp", None, None),
            P("head", "grp", None, None),
            P(("grp", "head"), None, None),
            P("head", "grp", None),
            P(None, "head", None),
            P(),
            P("head", "grp", None),
            P("head", "grp", None),
            P("head", None, None),
            P("head", None, None),
        ),
        out_specs=P("head", "grp", None),
        check_vma=False,
    )
```

profile of v0, /device:TPU:15, one launch (start us, length us, event | category | flops | bytes accessed | tf_op | source)
XLA Modules:
  0.0 386.3 jit_solution(4581564289091582553)
XLA Ops:
  9.7 6.5 %all-to-all-start.1 = ((bf16[128,16,512]{2,0,1:T(8,128)(2,1)}), bf16[128,16,512]{2,0,1:T(8,128)(2,1)}, u32[]{:S(2)}, u32[]{:S(2)}) async-start(bf16[128,16,512]{2,0,1:T(8,128)(2,1)} %bitcast.108), calls=%async_computation.1 | async-start | bytes 4194304 | tf_op jit(solution)/shard_map/all_to_all | solution.py:69
  18.5 33.3 %collective-permute-done.1 = bf16[512,512]{1,0:T(8,128)(2,1)S(1)} collective-permute-done((bf16[512,512]{1,0:T(8,128)(2,1)S(1)}, bf16[512,512]{1,0:T(8,128)(2,1)S(1)}, u32[]{:S(2)}, u32[]{:S(2)}) %collective-permute-start.1) | collective-permute-done | bytes 524320 | tf_op jit(solution)/shard_map/ppermute | solution.py:12
  52.8 4.1 %collective-permute-start.2 = (bf16[1024,512]{1,0:T(8,128)(2,1)}, bf16[1024,512]{1,0:T(8,128)(2,1)}, u32[]{:S(2)}, u32[]{:S(2)}) collective-permute-start(bf16[1024,512]{1,0:T(8,128)(2,1)} %pad_maximum_fusion.1), channel_id=1, source_target_pairs={{0,4},{1,5},{2,6},{3,7},{4,0},{5,1},{6,2},{7,3},{8,12},{9,13},{10,... | collective-permute-start | bytes 3145736 | tf_op jit(solution)/shard_map/ppermute | solution.py:12
  56.9 2.6 copy.42
  59.5 38.3 %all-to-all-done.1 = bf16[128,16,512]{2,0,1:T(8,128)(2,1)} async-done(((bf16[128,16,512]{2,0,1:T(8,128)(2,1)}), bf16[128,16,512]{2,0,1:T(8,128)(2,1)}, u32[]{:S(2)}, u32[]{:S(2)}) %all-to-all-start.1) | async-done | bytes 2097184 | tf_op jit(solution)/shard_map/all_to_all | solution.py:69
  97.7 4.4 %all-to-all-start = ((bf16[128,16,256]{2,0,1:T(8,128)(2,1)}), bf16[128,16,256]{2,0,1:T(8,128)(2,1)}, u32[]{:S(2)}, u32[]{:S(2)}) async-start(bf16[128,16,256]{2,0,1:T(8,128)(2,1)} %bitcast.95), calls=%async_computation | async-start | bytes 2097152 | tf_op jit(solution)/shard_map/all_to_all | solution.py:66
  102.2 20.2 %collective-permute-done.2 = bf16[1024,512]{1,0:T(8,128)(2,1)} collective-permute-done((bf16[1024,512]{1,0:T(8,128)(2,1)}, bf16[1024,512]{1,0:T(8,128)(2,1)}, u32[]{:S(2)}, u32[]{:S(2)}) %collective-permute-start.2) | collective-permute-done | bytes 1048608 | tf_op jit(solution)/shard_map/ppermute | solution.py:12
  124.9 3.0 fusion.57
  128.0 24.3 %all-to-all-done = bf16[128,16,256]{2,0,1:T(8,128)(2,1)} async-done(((bf16[128,16,256]{2,0,1:T(8,128)(2,1)}), bf16[128,16,256]{2,0,1:T(8,128)(2,1)}, u32[]{:S(2)}, u32[]{:S(2)}) %all-to-all-start) | async-done | bytes 1048608 | tf_op jit(solution)/shard_map/all_to_all | solution.py:66
  152.3 45.5 %while.11 = (s32[]{:T(128)}, bf16[4,512,256]{2,1,0:T(8,128)(2,1)}, s32[4]{0:T(128)S(1)}, bf16[2048,256]{1,0:T(8,128)(2,1)}, bf16[2048,256]{1,0:T(8,128)(2,1)S(1)...) while((s32[]{:T(128)}, bf16[4,512,256]{2,1,0:T(8,128)(2,1)}, ...), condition=%wide.region_5.6_spmd.clone, body=%wide.region_0.5_spmd.clone.sunk | while | flops 2164653568 | bytes 39617248 | solution.py:48
  155.4 2.3 fusion.81
  166.8 2.3 fusion.81
  178.2 2.3 fusion.81
  180.5 1.8 multiply_reduce_fusion.4
  189.6 2.3 fusion.81
  191.8 1.8 multiply_reduce_fusion.4
  198.3 2.7 reduce.2
  202.1 4.8 %all-to-all-start.2 = ((bf16[16,2,16384]{2,1,0:T(2,128)(2,1)}), bf16[16,2,16384]{2,1,0:T(2,128)(2,1)S(1)}, u32[]{:S(2)}, u32[]{:S(2)}) async-start(bf16[16,2,16384]{2,1,0:T(2,128)(2,1)} %reshape.162), calls=%async_computation.2 | async-start | bytes 2097152 | tf_op jit(solution)/shard_map/all_to_all | solution.py:77
  208.5 23.3 %all-to-all-done.2 = bf16[16,2,16384]{2,1,0:T(2,128)(2,1)S(1)} async-done(((bf16[16,2,16384]{2,1,0:T(2,128)(2,1)}), bf16[16,2,16384]{2,1,0:T(2,128)(2,1)S(1)}, u32[]{:S(2)}, u32[]{:S(2)}) %all-to-all-start.2) | async-done | bytes 1048608 | tf_op jit(solution)/shard_map/all_to_all | solution.py:77
  231.8 3.5 reshape.163
  235.2 2.8 copy.38
  238.0 8.6 %multiply_reduce_fusion.2 = (f32[128]{0:T(128)S(1)}, f32[128,2048]{1,0:T(8,128)S(1)}) fusion(bf16[128,16,256]{2,0,1:T(8,128)(2,1)} %bitcast.110, bf16[16,256,2048]{2,1,0:T(8,128)(2,1)} %all-gather.2.cloned.1.call-done, bf16[128,1,2048]{2,0,1:T(8,128)(2,1)} %param.15), kind=kOutput, calls=%fused_computation.46 | convolution fusion | flops 2148532224 | bytes 19399168 | tf_op jit(solution)/shard_map/rhi,hid->rd/dot_general | solution.py:86
  248.4 2.3 reshape.152
  250.6 4.4 %scatter_custom_fusion = bf16[512,2048]{1,0:T(8,128)(2,1)} fusion(s32[256]{0:T(256)S(1)} %bitcast.116, bf16[256,2048]{1,0:T(8,128)(2,1)} %reshape.152, bf16[]{:T(256)} %constant.7.clone.1), kind=kCustom, calls=%fused_computation.47 | custom fusion | bytes 2097664 | tf_op jit(solution)/shard_map/scatter | solution.py:105
  255.1 52.4 %all_to_all.66 = bf16[16,1,32,2048]{3,2,1,0:T(8,128)(2,1)S(1)} all-to-all(bf16[16,1,32,2048]{3,2,1,0:T(8,128)(2,1)} %bitcast.109), channel_id=1, replica_groups=mesh['grp'=2,'head'=16] {'head'}, dimensions={0} | all-to-all | bytes 4194304 | tf_op jit(solution)/shard_map/all_to_all | solution.py:110
  307.4 2.3 fusion.40
  309.8 2.6 fusion.36
  312.4 5.2 %all-to-all-start.4 = ((bf16[1,16,32,2048]{3,2,0,1:T(8,128)(2,1)}), bf16[1,16,32,2048]{3,2,0,1:T(8,128)(2,1)}, u32[]{:S(2)}, u32[]{:S(2)}) async-start(bf16[1,16,32,2048]{3,2,0,1:T(8,128)(2,1)} %fusion.36), calls=%async_computation.4 | async-start | bytes 4194304 | tf_op jit(solution)/shard_map/all_to_all | solution.py:120
  317.7 47.4 %all-to-all-done.4 = bf16[1,16,32,2048]{3,2,0,1:T(8,128)(2,1)} async-done(((bf16[1,16,32,2048]{3,2,0,1:T(8,128)(2,1)}), bf16[1,16,32,2048]{3,2,0,1:T(8,128)(2,1)}, u32[]{:S(2)}, u32[]{:S(2)}) %all-to-all-start.4) | async-done | bytes 2097184 | tf_op jit(solution)/shard_map/all_to_all | solution.py:120
  365.1 5.2 %gather_fusion = bf16[256,2048]{1,0:T(8,128)(2,1)} fusion(bf16[512,2048]{1,0:T(8,128)(2,1)} %bitcast.30, s32[1024]{0:T(1024)S(1)} %pad_clamp_fusion), kind=kCustom, calls=%fused_computation | custom fusion | bytes 2098176 | tf_op jit(solution)/shard_map/gather | solution.py:121
  370.3 3.4 reshape.139
  373.7 4.8 %multiply_reduce_fusion.1 = f32[128,2048]{1,0:T(8,128)S(1)} fusion(f32[128,2,2048]{2,1,0:T(2,128)} %reshape.139, f32[128,2]{1,0:T(8,128)S(1)} %copy.37), kind=kLoop, calls=%fused_computation.38 | loop fusion | flops 786432 | bytes 3146752 | tf_op jit(solution)/shard_map/reduce_sum | solution.py:123
  (93 shorter events, 39.9 us)
Async XLA Ops:
  6.5 303.3 %copy-start = (bf16[1,512,2048]{2,1,0:T(8,128)(2,1)S(1)}, bf16[1,512,2048]{2,1,0:T(8,128)(2,1)}, u32[]{:S(2)}) copy-start(bf16[1,512,2048]{2,1,0:T(8,128)(2,1)} %param.21) | copy-start | bytes 6291460
  6.5 9.7 %copy-start.1 = (bf16[1,256,512]{2,1,0:T(8,128)(2,1)S(1)}, bf16[1,256,512]{2,1,0:T(8,128)(2,1)}, u32[]{:S(2)}) copy-start(bf16[1,256,512]{2,1,0:T(8,128)(2,1)} %param.14) | copy-start | bytes 786436
  6.5 231.4 %all-gather.2.cloned.1.call-start = ((), (), s32[]{:S(2)}) async-start(), calls=%async_computation.5 | async-start | bytes 17825792 | tf_op jit(solution)/shard_map/all_gather | solution.py:89
  9.7 88.0 %all-to-all-start.1 = ((bf16[128,16,512]{2,0,1:T(8,128)(2,1)}), bf16[128,16,512]{2,0,1:T(8,128)(2,1)}, u32[]{:S(2)}, u32[]{:S(2)}) async-start(bf16[128,16,512]{2,0,1:T(8,128)(2,1)} %bitcast.108), calls=%async_computation.1 | async-start | bytes 4194304 | tf_op jit(solution)/shard_map/all_to_all | solution.py:69
  16.3 1.8 collective-permute-start
  18.1 33.7 %collective-permute-start.1 = (bf16[512,512]{1,0:T(8,128)(2,1)S(1)}, bf16[512,512]{1,0:T(8,128)(2,1)S(1)}, u32[]{:S(2)}, u32[]{:S(2)}) collective-permute-start(bf16[512,512]{1,0:T(8,128)(2,1)S(1)} %pad_maximum_fusion.2), channel_id=1, source_target_pairs={{0,2},{1,3},{2,0},{3,1},{4,6},{5,7},{6,4},{7,5},{8,10},{9,11},{10,... | collective-permute-start | bytes 1572872 | tf_op jit(solution)/shard_map/ppermute | solution.py:12
  52.8 69.6 %collective-permute-start.2 = (bf16[1024,512]{1,0:T(8,128)(2,1)}, bf16[1024,512]{1,0:T(8,128)(2,1)}, u32[]{:S(2)}, u32[]{:S(2)}) collective-permute-start(bf16[1024,512]{1,0:T(8,128)(2,1)} %pad_maximum_fusion.1), channel_id=1, source_target_pairs={{0,4},{1,5},{2,6},{3,7},{4,0},{5,1},{6,2},{7,3},{8,12},{9,13},{10,... | collective-permute-start | bytes 3145736 | tf_op jit(solution)/shard_map/ppermute | solution.py:12
  97.7 54.5 %all-to-all-start = ((bf16[128,16,256]{2,0,1:T(8,128)(2,1)}), bf16[128,16,256]{2,0,1:T(8,128)(2,1)}, u32[]{:S(2)}, u32[]{:S(2)}) async-start(bf16[128,16,256]{2,0,1:T(8,128)(2,1)} %bitcast.95), calls=%async_computation | async-start | bytes 2097152 | tf_op jit(solution)/shard_map/all_to_all | solution.py:66
  159.5 1.4 copy-start.2
  160.9 1.2 copy-start.3
  170.9 1.4 copy-start.2
  172.3 1.2 copy-start.3
  182.3 1.4 copy-start.2
  183.7 1.2 copy-start.3
  193.7 1.4 copy-start.2
  195.1 1.2 copy-start.3
  197.8 9.1 %copy-start.5 = (s32[128,1,2]{0,2,1:T(2,128)S(1)}, s32[128,1,2]{0,2,1:T(2,128)}, u32[]{:S(2)}) copy-start(s32[128,1,2]{0,2,1:T(2,128)} %param.18) | copy-start | bytes 3076
  202.1 29.7 %all-to-all-start.2 = ((bf16[16,2,16384]{2,1,0:T(2,128)(2,1)}), bf16[16,2,16384]{2,1,0:T(2,128)(2,1)S(1)}, u32[]{:S(2)}, u32[]{:S(2)}) async-start(bf16[16,2,16384]{2,1,0:T(2,128)(2,1)} %reshape.162), calls=%async_computation.2 | async-start | bytes 2097152 | tf_op jit(solution)/shard_map/all_to_all | solution.py:77
  238.0 8.6 %copy-start.4 = (f32[2048]{0:T(1024)S(1)}, f32[2048]{0:T(1024)}, u32[]{:S(2)}) copy-start(f32[2048]{0:T(1024)} %param.17) | copy-start | bytes 24580
  255.1 52.4 %copy-start.7 = (bf16[1,2048,1024]{2,1,0:T(8,128)(2,1)S(1)}, bf16[1,2048,1024]{2,1,0:T(8,128)(2,1)}, u32[]{:S(2)}) copy-start(bf16[1,2048,1024]{2,1,0:T(8,128)(2,1)} %param.20) | copy-start | bytes 12582916
  312.4 5.2 %copy-start.6 = (f32[128,1,2]{0,2,1:T(2,128)S(1)}, f32[128,1,2]{0,2,1:T(2,128)}, u32[]{:S(2)}) copy-start(f32[128,1,2]{0,2,1:T(2,128)} %param.19) | copy-start | bytes 3076
  312.4 52.7 %all-to-all-start.4 = ((bf16[1,16,32,2048]{3,2,0,1:T(8,128)(2,1)}), bf16[1,16,32,2048]{3,2,0,1:T(8,128)(2,1)}, u32[]{:S(2)}, u32[]{:S(2)}) async-start(bf16[1,16,32,2048]{3,2,0,1:T(8,128)(2,1)} %fusion.36), calls=%async_computation.4 | async-start | bytes 4194304 | tf_op jit(solution)/shard_map/all_to_all | solution.py:120
Sparse Core Ops, SparseCore 0:
  9.5 185.4 all-gather.1
where the time goes:
time: 388 us; the launch traced here: 386 us
  waiting for transfers between devices  189 us (49%)
  blocking collectives  52.4 us (14%)
  matrix products  39.2 us (10%)
  local copies, waits for them, and re-layouts  38.8 us (10%)
  starting transfers between devices  25.8 us (7%)
  other arithmetic  19.9 us (5%)
  between operations  13.5 us (3%)
  loops' own time  7.86 us (2%)
    ppermute x3, waiting for transfers between devices, partner_2(): return lax.ppermute(value, axis, pairs)  54.9 us
    all_to_all x1, blocking collectives, local(): lax.all_to_all(outgoing, 'head', split_axis=0, concat_axis=1, tiled=True)  52.4 us
    all_to_all x1, waiting for transfers between devices, local(): lax.all_to_all(answered, 'head', split_axis=1, concat_axis=0, tiled=True)  47.4 us
    all_to_all x1, waiting for transfers between devices, local(): lax.all_to_all(pair_slots, 'head', split_axis=1, concat_axis=0, tiled=True)  38.3 us
    all_to_all x1, waiting for transfers between devices, local(): lax.all_to_all(query_slots, 'head', split_axis=1, concat_axis=0, tiled=True)  24.3 us
    all_to_all x1, waiting for transfers between devices, local(): lax.all_to_all(attended.reshape(attended.shape[0], 1, head_width), 'head'...  23.3 us
    unnamed x17, local copies, waits for them, and re-layouts  10 us
    dot_general x4, matrix products, one_block(): jnp.dot(query_rows, new_keys.T, preferred_element_type=jnp.float32)  9.17 us
  transfers between devices with their start and end apart: 8, of which 7 were waited for; matrix products, arithmetic and copies ran while one was open for 16% of the time, Pallas kernels for 0%

commit v1 on v0

--- a/solution.py
+++ b/solution.py
@@ -4,6 +4,13 @@
 from jax.sharding import PartitionSpec as P
 
 eps_norm = 1e-06
+
+
+def trade_parts(x, axis, split, join):
+    count = lax.axis_size(axis)
+    blocks = jnp.stack(jnp.split(x, count, axis=split), axis=0)
+    blocks = lax.all_to_all(blocks, axis, split_axis=0, concat_axis=0)
+    return jnp.concatenate(blocks, axis=join)
 
 
 def partner_2(value, axis, stride):
@@ -63,9 +70,7 @@
         new_kv[:, :, :, None, :], (local_rows, seq_count, pair_heads, group_size, 2 * head_width)
     )
     pair_slots = pair_slots.reshape(local_rows, axis_count, 2 * head_width)
-    head_queries = lax.all_to_all(query_slots, "head", split_axis=1, concat_axis=0, tiled=True)[
-        :, 0
-    ]
+    head_queries = trade_parts(query_slots, "head", 1, 0)[:, 0]
     head_pairs = lax.all_to_all(pair_slots, "head", split_axis=1, concat_axis=0, tiled=True)[:, 0]
     cache_rows = cache[0]
     for bit_number in range(group_size.bit_length() - 1):

time: 388 us -> 386 us (level)
  waiting for transfers between devices: 189 us -> 180 us
  local copies, waits for them, and re-layouts: 38.8 us -> 47.7 us
    ppermute x3, waiting for transfers between devices: 54.9 us -> 44.6 us  [partner_2(): return lax.ppermute(value, axis, pairs)]
    unnamed x17 -> x32, local copies, waits for them, and re-layouts: 10 us -> 18.4 us
  transfers between devices with their start and end apart: 8 -> 8, of which waited for: 7 -> 6; matrix products, arithmetic and copies ran while one was open for 16% -> 18% of each run, Pallas kernels for 0% -> 0%
where the time goes in v1:
time: 386 us; the launch traced here: 385 us
  waiting for transfers between devices  180 us (47%)
  blocking collectives  52.3 us (14%)
  local copies, waits for them, and re-layouts  47.7 us (12%)
  matrix products  39.1 us (10%)
  starting transfers between devices  25.8 us (7%)
  other arithmetic  19.6 us (5%)
  between operations  13.5 us (3%)
  loops' own time  6.95 us (2%)
    all_to_all x1, blocking collectives, local(): lax.all_to_all(outgoing, 'head', split_axis=0, concat_axis=1, tiled=True)  52.3 us
    all_to_all x1, waiting for transfers between devices, local(): lax.all_to_all(answered, 'head', split_axis=1, concat_axis=0, tiled=True)  47.4 us
    ppermute x3, waiting for transfers between devices, partner_2(): return lax.ppermute(value, axis, pairs)  44.6 us
    all_to_all x1, waiting for transfers between devices, local(): lax.all_to_all(pair_slots, 'head', split_axis=1, concat_axis=0, tiled=True)  39.6 us
    all_to_all x1, waiting for transfers between devices, trade_parts(): blocks = lax.all_to_all(blocks, axis, split_axis=0, concat_axis=0)  24.3 us
    all_to_all x1, waiting for transfers between devices, local(): lax.all_to_all(attended.reshape(attended.shape[0], 1, head_width), 'head'...  23.3 us
    unnamed x32, local copies, waits for them, and re-layouts  18.4 us
    dot_general x4, matrix products, one_block(): jnp.dot(query_rows, new_keys.T, preferred_element_type=jnp.float32)  9.17 us
  transfers between devices with their start and end apart: 8, of which 6 were waited for; matrix products, arithmetic and copies ran while one was open for 18% of the time, Pallas kernels for 0%

profile of v1, /device:TPU:15, one launch (start us, length us, event | category | flops | bytes accessed | tf_op | source)
XLA Modules:
  0.0 384.9 jit_solution(2189478793001961747)
XLA Ops:
  9.7 6.5 %all-to-all-start.1 = ((bf16[128,16,512]{2,0,1:T(8,128)(2,1)}), bf16[128,16,512]{2,0,1:T(8,128)(2,1)}, u32[]{:S(2)}, u32[]{:S(2)}) async-start(bf16[128,16,512]{2,0,1:T(8,128)(2,1)} %bitcast.168), calls=%async_computation.1 | async-start | bytes 4194304 | tf_op jit(solution)/shard_map/all_to_all | solution.py:74
  27.4 24.4 %collective-permute-done.1 = bf16[512,512]{1,0:T(8,128)(2,1)S(1)} collective-permute-done((bf16[512,512]{1,0:T(8,128)(2,1)S(1)}, bf16[512,512]{1,0:T(8,128)(2,1)S(1)}, u32[]{:S(2)}, u32[]{:S(2)}) %collective-permute-start.1) | collective-permute-done | bytes 524320 | tf_op jit(solution)/shard_map/ppermute | solution.py:19
  52.8 4.1 %collective-permute-start.2 = (bf16[1024,512]{1,0:T(8,128)(2,1)}, bf16[1024,512]{1,0:T(8,128)(2,1)}, u32[]{:S(2)}, u32[]{:S(2)}) collective-permute-start(bf16[1024,512]{1,0:T(8,128)(2,1)} %pad_maximum_fusion.1), channel_id=1, source_target_pairs={{0,4},{1,5},{2,6},{3,7},{4,0},{5,1},{6,2},{7,3},{8,12},{9,13},{10,... | collective-permute-start | bytes 3145736 | tf_op jit(solution)/shard_map/ppermute | solution.py:19
  58.2 39.6 %all-to-all-done.1 = bf16[128,16,512]{2,0,1:T(8,128)(2,1)} async-done(((bf16[128,16,512]{2,0,1:T(8,128)(2,1)}), bf16[128,16,512]{2,0,1:T(8,128)(2,1)}, u32[]{:S(2)}, u32[]{:S(2)}) %all-to-all-start.1) | async-done | bytes 2097184 | tf_op jit(solution)/shard_map/all_to_all | solution.py:74
  97.7 4.4 %all-to-all-start = ((bf16[16,128,1,256]{3,1,2,0:T(8,128)(2,1)}), bf16[16,128,1,256]{3,1,2,0:T(8,128)(2,1)}, u32[]{:S(2)}, u32[]{:S(2)}) async-start(bf16[16,128,1,256]{3,1,2,0:T(8,128)(2,1)} %fusion.51), calls=%async_computation | async-start | bytes 2097152 | tf_op jit(solution)/shard_map/all_to_all | solution.py:12
  102.2 20.2 %collective-permute-done.2 = bf16[1024,512]{1,0:T(8,128)(2,1)} collective-permute-done((bf16[1024,512]{1,0:T(8,128)(2,1)}, bf16[1024,512]{1,0:T(8,128)(2,1)}, u32[]{:S(2)}, u32[]{:S(2)}) %collective-permute-start.2) | collective-permute-done | bytes 1048608 | tf_op jit(solution)/shard_map/ppermute | solution.py:19
  124.9 3.0 fusion.73
  128.0 24.3 %all-to-all-done = bf16[16,128,1,256]{3,1,2,0:T(8,128)(2,1)} async-done(((bf16[16,128,1,256]{3,1,2,0:T(8,128)(2,1)}), bf16[16,128,1,256]{3,1,2,0:T(8,128)(2,1)}, u32[]{:S(2)}, u32[]{:S(2)}) %all-to-all-start) | async-done | bytes 1048608 | tf_op jit(solution)/shard_map/all_to_all | solution.py:12
  152.3 44.2 %while.11 = (s32[]{:T(128)}, bf16[4,512,256]{2,1,0:T(8,128)(2,1)}, s32[4]{0:T(128)S(1)}, bf16[2048,256]{1,0:T(8,128)(2,1)}, bf16[2048,256]{1,0:T(8,128)(2,1)S(1)...) while((s32[]{:T(128)}, bf16[4,512,256]{2,1,0:T(8,128)(2,1)}, ...), condition=%wide.region_5.6_spmd.clone, body=%wide.region_0.5_spmd.clone.sunk | while | flops 2164653568 | bytes 39617248 | solution.py:55
  155.1 2.3 fusion.97
  157.4 1.8 multiply_reduce_fusion.4
  166.1 2.3 fusion.97
  168.4 1.8 multiply_reduce_fusion.4
  177.2 2.3 fusion.97
  179.5 1.8 multiply_reduce_fusion.4
  188.2 2.3 fusion.97
  196.9 2.7 reduce.2
  200.7 4.8 %all-to-all-start.2 = ((bf16[16,2,16384]{2,1,0:T(2,128)(2,1)}), bf16[16,2,16384]{2,1,0:T(2,128)(2,1)S(1)}, u32[]{:S(2)}, u32[]{:S(2)}) async-start(bf16[16,2,16384]{2,1,0:T(2,128)(2,1)} %reshape.161), calls=%async_computation.2 | async-start | bytes 2097152 | tf_op jit(solution)/shard_map/all_to_all | solution.py:82
  207.2 23.3 %all-to-all-done.2 = bf16[16,2,16384]{2,1,0:T(2,128)(2,1)S(1)} async-done(((bf16[16,2,16384]{2,1,0:T(2,128)(2,1)}), bf16[16,2,16384]{2,1,0:T(2,128)(2,1)S(1)}, u32[]{:S(2)}, u32[]{:S(2)}) %all-to-all-start.2) | async-done | bytes 1048608 | tf_op jit(solution)/shard_map/all_to_all | solution.py:82
  230.4 3.5 reshape.162
  233.9 2.8 copy.52
  236.7 8.6 %multiply_reduce_fusion.2 = (f32[128]{0:T(128)S(1)}, f32[128,2048]{1,0:T(8,128)S(1)}) fusion(bf16[128,16,256]{2,0,1:T(8,128)(2,1)} %bitcast.170, bf16[16,256,2048]{2,1,0:T(8,128)(2,1)} %all-gather.2.cloned.1.call-done, bf16[128,1,2048]{2,0,1:T(8,128)(2,1)} %param.15), kind=kOutput, calls=%fused_computation.46 | convolution fusion | flops 2148532224 | bytes 19399168 | tf_op jit(solution)/shard_map/rhi,hid->rd/dot_general | solution.py:91
  247.1 2.3 reshape.151
  249.3 4.4 %scatter_custom_fusion = bf16[512,2048]{1,0:T(8,128)(2,1)} fusion(s32[256]{0:T(256)S(1)} %bitcast.192, bf16[256,2048]{1,0:T(8,128)(2,1)} %reshape.151, bf16[]{:T(256)} %constant.7.clone.1), kind=kCustom, calls=%fused_computation.47 | custom fusion | bytes 2097664 | tf_op jit(solution)/shard_map/scatter | solution.py:110
  253.7 52.3 %all_to_all.56 = bf16[16,1,32,2048]{3,2,1,0:T(8,128)(2,1)S(1)} all-to-all(bf16[16,1,32,2048]{3,2,1,0:T(8,128)(2,1)} %bitcast.169), channel_id=1, replica_groups=mesh['grp'=2,'head'=16] {'head'}, dimensions={0} | all-to-all | bytes 4194304 | tf_op jit(solution)/shard_map/all_to_all | solution.py:115
  306.1 2.3 fusion.40
  308.4 2.6 fusion.36
  311.0 5.2 %all-to-all-start.4 = ((bf16[1,16,32,2048]{3,2,0,1:T(8,128)(2,1)}), bf16[1,16,32,2048]{3,2,0,1:T(8,128)(2,1)}, u32[]{:S(2)}, u32[]{:S(2)}) async-start(bf16[1,16,32,2048]{3,2,0,1:T(8,128)(2,1)} %fusion.36), calls=%async_computation.4 | async-start | bytes 4194304 | tf_op jit(solution)/shard_map/all_to_all | solution.py:125
  316.3 47.4 %all-to-all-done.4 = bf16[1,16,32,2048]{3,2,0,1:T(8,128)(2,1)} async-done(((bf16[1,16,32,2048]{3,2,0,1:T(8,128)(2,1)}), bf16[1,16,32,2048]{3,2,0,1:T(8,128)(2,1)}, u32[]{:S(2)}, u32[]{:S(2)}) %all-to-all-start.4) | async-done | bytes 2097184 | tf_op jit(solution)/shard_map/all_to_all | solution.py:125
  363.7 5.2 %gather_fusion = bf16[256,2048]{1,0:T(8,128)(2,1)} fusion(bf16[512,2048]{1,0:T(8,128)(2,1)} %bitcast.44, s32[1024]{0:T(1024)S(1)} %pad_clamp_fusion), kind=kCustom, calls=%fused_computation | custom fusion | bytes 2098176 | tf_op jit(solution)/shard_map/gather | solution.py:126
  368.9 3.4 reshape.138
  372.3 4.8 %multiply_reduce_fusion.1 = f32[128,2048]{1,0:T(8,128)S(1)} fusion(f32[128,2,2048]{2,1,0:T(2,128)} %reshape.138, f32[128,2]{1,0:T(8,128)S(1)} %copy.51), kind=kLoop, calls=%fused_computation.38 | loop fusion | flops 786432 | bytes 3146752 | tf_op jit(solution)/shard_map/reduce_sum | solution.py:128
  (109 shorter events, 47.8 us)
Async XLA Ops:
  6.5 301.9 %copy-start = (bf16[1,512,2048]{2,1,0:T(8,128)(2,1)S(1)}, bf16[1,512,2048]{2,1,0:T(8,128)(2,1)}, u32[]{:S(2)}) copy-start(bf16[1,512,2048]{2,1,0:T(8,128)(2,1)} %param.21) | copy-start | bytes 6291460
  6.5 9.7 %copy-start.1 = (bf16[1,256,512]{2,1,0:T(8,128)(2,1)S(1)}, bf16[1,256,512]{2,1,0:T(8,128)(2,1)}, u32[]{:S(2)}) copy-start(bf16[1,256,512]{2,1,0:T(8,128)(2,1)} %param.14) | copy-start | bytes 786436
  6.5 230.1 %all-gather.2.cloned.1.call-start = ((), (), s32[]{:S(2)}) async-start(), calls=%async_computation.5 | async-start | bytes 17825792 | tf_op jit(solution)/shard_map/all_gather | solution.py:94
  9.7 88.0 %all-to-all-start.1 = ((bf16[128,16,512]{2,0,1:T(8,128)(2,1)}), bf16[128,16,512]{2,0,1:T(8,128)(2,1)}, u32[]{:S(2)}, u32[]{:S(2)}) async-start(bf16[128,16,512]{2,0,1:T(8,128)(2,1)} %bitcast.168), calls=%async_computation.1 | async-start | bytes 4194304 | tf_op jit(solution)/shard_map/all_to_all | solution.py:74
  16.3 8.9 %collective-permute-start = (bf16[256,512]{1,0:T(8,128)(2,1)S(1)}, bf16[256,512]{1,0:T(8,128)(2,1)S(1)}, u32[]{:S(2)}, u32[]{:S(2)}) collective-permute-start(bf16[256,512]{1,0:T(8,128)(2,1)S(1)} %bitcast.187), channel_id=1, source_target_pairs={{0,1},{1,0},{2,3},{3,2},{4,5},{5,4},{6,7},{7,6},{8,9},{9,8},{10,11... | collective-permute-start | bytes 786440 | tf_op jit(solution)/shard_map/ppermute | solution.py:19
  25.2 26.6 %collective-permute-start.1 = (bf16[512,512]{1,0:T(8,128)(2,1)S(1)}, bf16[512,512]{1,0:T(8,128)(2,1)S(1)}, u32[]{:S(2)}, u32[]{:S(2)}) collective-permute-start(bf16[512,512]{1,0:T(8,128)(2,1)S(1)} %pad_maximum_fusion.2), channel_id=1, source_target_pairs={{0,2},{1,3},{2,0},{3,1},{4,6},{5,7},{6,4},{7,5},{8,10},{9,11},{10,... | collective-permute-start | bytes 1572872 | tf_op jit(solution)/shard_map/ppermute | solution.py:19
  52.8 69.6 %collective-permute-start.2 = (bf16[1024,512]{1,0:T(8,128)(2,1)}, bf16[1024,512]{1,0:T(8,128)(2,1)}, u32[]{:S(2)}, u32[]{:S(2)}) collective-permute-start(bf16[1024,512]{1,0:T(8,128)(2,1)} %pad_maximum_fusion.1), channel_id=1, source_target_pairs={{0,4},{1,5},{2,6},{3,7},{4,0},{5,1},{6,2},{7,3},{8,12},{9,13},{10,... | collective-permute-start | bytes 3145736 | tf_op jit(solution)/shard_map/ppermute | solution.py:19
  97.7 54.5 %all-to-all-start = ((bf16[16,128,1,256]{3,1,2,0:T(8,128)(2,1)}), bf16[16,128,1,256]{3,1,2,0:T(8,128)(2,1)}, u32[]{:S(2)}, u32[]{:S(2)}) async-start(bf16[16,128,1,256]{3,1,2,0:T(8,128)(2,1)} %fusion.51), calls=%async_computation | async-start | bytes 2097152 | tf_op jit(solution)/shard_map/all_to_all | solution.py:12
  159.2 1.4 copy-start.2
  160.6 1.2 copy-start.3
  170.2 1.4 copy-start.2
  171.6 1.2 copy-start.3
  181.3 1.4 copy-start.2
  182.6 1.2 copy-start.3
  192.3 1.4 copy-start.2
  193.7 1.2 copy-start.3
  196.4 9.2 %copy-start.5 = (s32[128,1,2]{0,2,1:T(2,128)S(1)}, s32[128,1,2]{0,2,1:T(2,128)}, u32[]{:S(2)}) copy-start(s32[128,1,2]{0,2,1:T(2,128)} %param.18) | copy-start | bytes 3076
  200.7 29.7 %all-to-all-start.2 = ((bf16[16,2,16384]{2,1,0:T(2,128)(2,1)}), bf16[16,2,16384]{2,1,0:T(2,128)(2,1)S(1)}, u32[]{:S(2)}, u32[]{:S(2)}) async-start(bf16[16,2,16384]{2,1,0:T(2,128)(2,1)} %reshape.161), calls=%async_computation.2 | async-start | bytes 2097152 | tf_op jit(solution)/shard_map/all_to_all | solution.py:82
  236.7 8.6 %copy-start.4 = (f32[2048]{0:T(1024)S(1)}, f32[2048]{0:T(1024)}, u32[]{:S(2)}) copy-start(f32[2048]{0:T(1024)} %param.17) | copy-start | bytes 24580
  253.7 52.3 %copy-start.7 = (bf16[1,2048,1024]{2,1,0:T(8,128)(2,1)S(1)}, bf16[1,2048,1024]{2,1,0:T(8,128)(2,1)}, u32[]{:S(2)}) copy-start(bf16[1,2048,1024]{2,1,0:T(8,128)(2,1)} %param.20) | copy-start | bytes 12582916
  311.0 5.2 %copy-start.6 = (f32[128,1,2]{0,2,1:T(2,128)S(1)}, f32[128,1,2]{0,2,1:T(2,128)}, u32[]{:S(2)}) copy-start(f32[128,1,2]{0,2,1:T(2,128)} %param.19) | copy-start | bytes 3076
  311.0 52.7 %all-to-all-start.4 = ((bf16[1,16,32,2048]{3,2,0,1:T(8,128)(2,1)}), bf16[1,16,32,2048]{3,2,0,1:T(8,128)(2,1)}, u32[]{:S(2)}, u32[]{:S(2)}) async-start(bf16[1,16,32,2048]{3,2,0,1:T(8,128)(2,1)} %fusion.36), calls=%async_computation.4 | async-start | bytes 4194304 | tf_op jit(solution)/shard_map/all_to_all | solution.py:125
Sparse Core Ops, SparseCore 0:
  9.5 185.4 all-gather.1
